TPU v7x, 256 devices: a whole 4x4x8 slice. The times are simulated.
256 devices in a mesh: replica: 8 (over z), tile: 32 (over y, x, core).
Axes of the slice: x: 4, y: 4, z: 8, core: 2. Of those that a mesh axis runs over, the one named last changes fastest.
Arguments:
- fields: bfloat16 [8, 64, 128, 8, 128], P('replica', None, 'tile'), may hold values from -6 to 6
- convolution_weight: bfloat16 [64, 1728], replicated, may hold values from -0.15625 to 0.15625
- convolution_bias: float32 [64], replicated, may hold values from -3 to 3
- query_owner: int32 [8, 4096, 1], P('replica', 'tile'), may hold values from 0 to 31; in each aligned block of 128 rows (0 to 127, 128 to 255, ..., all dimensions but the last counted through in order) at most 8 rows name the same one
- query_cell: int32 [8, 4096], P('replica', 'tile'), may hold values from 0 to 4095
- query_frac: float32 [8, 3, 4096], P('replica', None, 'tile'), may hold values from 0 to 1
- target: float32 [8, 5, 4096], P('replica', None, 'tile'), may hold values from -6 to 6
- w_latent: float32 [64, 512], replicated, may hold values from -3 to 3
- w_pos: float32 [3, 512], replicated, may hold values from -3.5 to 3.5
- bias_one: float32 [512], replicated, may hold values from -2 to 2
- w_mid: float32 [512, 512], replicated, may hold values from -0.5 to 0.5
- bias_two: float32 [512], replicated, may hold values from -2 to 2
- w_out: float32 [5, 512], replicated, may hold values from -0.25 to 0.25
- bias_out: float32 [5], replicated, may hold values from -3 to 3
Outputs:
- prediction: float32 [8, 5, 4096], P('replica', None, 'tile')
- grad_latent: float32 [64, 512], replicated
- grad_pos: float32 [3, 512], replicated
- grad_bias_one: float32 [512], replicated
- grad_mid: float32 [512, 512], replicated
- grad_bias_two: float32 [512], replicated
- grad_out: float32 [5, 512], replicated
- grad_bias_out: float32 [5], replicated
- loss: float32 [], replicated
Inputs may be any that keep to these rules, and one draw needn't show every extreme that they name: `query_owner`: among the query points of one device, no tile is named more than 8 times; in every draw some device names some tile exactly 8 times.
All inputs are finite; a program needn't handle non-finite values.
Results may differ from a plain program's by a relative error of at most 0.0009.
The roundings to bfloat16 on the way count: a program that leaves them out, or rounds other values in their place, can miss the bound.
Values may be sent and summed in bfloat16 or wider, within the bound.
A program may use at most 64 MiB of HBM per device.

v0:
```python
import jax
import jax.numpy as jnp
from jax import lax
from jax.sharding import PartitionSpec as P

DILATION_RATE = 2
VISCOSITY = 0.05
DIFFUSIVITY = 0.05
RESIDUAL_WEIGHT = 0.5


def extended_2(cells, sides, width):
    for axis, dim in sides:
        count = lax.axis_size(axis)
        head = lax.slice_in_dim(cells, 0, width, axis=dim)
        tail = lax.slice_in_dim(cells, cells.shape[dim] - width, cells.shape[dim], axis=dim)
        cells = jnp.concatenate(
            [
                lax.ppermute(tail, axis, [(i, (i + 1) % count) for i in range(count)]),
                cells,
                lax.ppermute(head, axis, [((i + 1) % count, i) for i in range(count)]),
            ],
            axis=dim,
        )
    return cells


def passed_along(value, axis, steps):
    count = lax.axis_size(axis)
    pairs = [(source, (source + steps) % count) for source in range(count)]
    return lax.ppermute(value, axis, pairs)


def corner_index(start_x, start_y, start_z, span_x, span_y, span_z):
    listed = []
    for corner in range(8):
        high_x = corner // 4
        high_y = corner // 2 % 2
        high_z = corner % 2
        listed.append(
            (start_x + high_x) % span_x * (span_y * span_z)
            + (start_y + high_y) % span_y * span_z
            + (start_z + high_z) % span_z
        )
    return jnp.stack(listed, axis=0)


def corner_weight(fraction):
    frac_x, frac_y, frac_z = (fraction[0], fraction[1], fraction[2])
    listed = []
    for corner in range(8):
        part_x = frac_x if corner // 4 == 1 else 1.0 - frac_x
        part_y = frac_y if corner // 2 % 2 == 1 else 1.0 - frac_y
        part_z = frac_z if corner % 2 == 1 else 1.0 - frac_z
        listed.append(part_x * part_y * part_z)
    return jnp.stack(listed, axis=0).astype(jnp.bfloat16)


def tanh_jet(pre_act, tangent, second):
    activation = jnp.tanh(pre_act)
    slope_one = 1.0 - activation * activation
    curvature = -2.0 * activation * slope_one
    return (
        activation,
        slope_one[None] * tangent,
        slope_one[None] * second + curvature[None] * tangent * tangent,
    )


def decode(params, latent_code, position):
    w_latent, w_pos, bias_one, w_mid, bias_two, w_out, bias_out = params
    highest = lax.Precision.HIGHEST
    row_count = latent_code.shape[0]
    hidden_width = w_mid.shape[0]
    first_sum = (
        jnp.dot(latent_code, w_latent, precision=highest)
        + jnp.dot(position, w_pos, precision=highest)
        + bias_one
    )
    tangent = jnp.broadcast_to(w_pos[:, None, :], (3, row_count, hidden_width))
    second = jnp.zeros((3, row_count, hidden_width), jnp.float32)
    activation, tangent, second = tanh_jet(first_sum, tangent, second)
    stacked = jnp.concatenate([activation[None], tangent, second], axis=0).reshape(
        7 * row_count, hidden_width
    )
    mixed_jet = jnp.dot(stacked, w_mid, precision=highest).reshape(7, row_count, hidden_width)
    activation, tangent, second = tanh_jet(mixed_jet[0] + bias_two, mixed_jet[1:4], mixed_jet[4:7])
    stacked = jnp.concatenate([activation[None], tangent, second], axis=0).reshape(
        7 * row_count, hidden_width
    )
    result_jet = jnp.dot(stacked, w_out.T, precision=highest).reshape(7, row_count, 5)
    return (result_jet[0] + bias_out, result_jet[1:4], result_jet[4:7])


def point_loss(params, latent_code, position, target_rows, query_total):
    value, first_jet, second_jet = decode(params, latent_code, position)
    laplace = jnp.sum(second_jet, axis=0)
    velocity = value[:, 2:5]
    advection = jnp.sum(velocity.T[:, :, None] * first_jet, axis=0)
    continuity = first_jet[0][:, 2] + first_jet[1][:, 3] + first_jet[2][:, 4]
    pressure = jnp.stack([first_jet[0][:, 1], first_jet[1][:, 1], first_jet[2][:, 1]], axis=1)
    momentum = advection[:, 2:5] + pressure - VISCOSITY * laplace[:, 2:5]
    momentum = momentum - jnp.concatenate([jnp.zeros_like(value[:, :2]), value[:, 0:1]], axis=1)
    energy = advection[:, 0] - DIFFUSIVITY * laplace[:, 0]
    misfit = jnp.sum((value - target_rows) * (value - target_rows), axis=1)
    physics = continuity * continuity + jnp.sum(momentum * momentum, axis=1) + energy * energy
    return (jnp.sum(misfit + RESIDUAL_WEIGHT * physics) / query_total, value)


def convolved_tile(padded_field, convolution_weight, convolution_bias, border_width, out_planes):
    channels, rows_y, rows_z = (padded_field.shape[0], padded_field.shape[2], padded_field.shape[3])
    summed = jnp.zeros((channels, out_planes * rows_y * rows_z), jnp.float32)
    for spacing_along_y in (-1, 0, 1):
        for spacing_along_z in (-1, 0, 1):
            shifted_field = jnp.roll(
                padded_field, (-spacing_along_y, -spacing_along_z), axis=(2, 3)
            )
            for spacing_along_x in (-1, 0, 1):
                tap_index = (
                    9 * (spacing_along_x + 1) + 3 * (spacing_along_y + 1) + spacing_along_z + 1
                )
                leading_plane = border_width + DILATION_RATE * spacing_along_x
                plane_slab = shifted_field[:, leading_plane : leading_plane + out_planes].reshape(
                    channels, out_planes * rows_y * rows_z
                )
                summed = summed + jnp.dot(
                    convolution_weight[:, tap_index * channels : (tap_index + 1) * channels],
                    plane_slab,
                    preferred_element_type=jnp.float32,
                )
    latent_code = jax.nn.gelu(summed + convolution_bias[:, None]).astype(jnp.bfloat16)
    return latent_code.reshape(channels, out_planes, rows_y, rows_z)


def body(
    fields,
    convolution_weight,
    convolution_bias,
    query_owner,
    query_cell,
    query_frac,
    target,
    w_latent,
    w_pos,
    bias_one,
    w_mid,
    bias_two,
    w_out,
    bias_out,
):
    tile_count = lax.axis_size("tile")
    replica_count = lax.axis_size("replica")
    channels, plane_list, rows_y, rows_z = (
        fields.shape[1],
        fields.shape[2],
        fields.shape[3],
        fields.shape[4],
    )
    local_field = fields[0]
    padded_field = extended_2(local_field, (("tile", 1),), DILATION_RATE)
    latent_code = convolved_tile(
        padded_field, convolution_weight, convolution_bias, DILATION_RATE, plane_list
    )
    upper_plane = passed_along(latent_code[:, :1], "tile", -1)
    extended = jnp.concatenate([latent_code, upper_plane], axis=1)
    plane_span = extended.shape[1]
    flat_latent = extended.reshape(channels, plane_span * rows_y * rows_z)
    owner_tile = query_owner[0, :, 0]
    base_cell = query_cell[0]
    fraction = query_frac[0]
    query_count = owner_tile.shape[0]
    slot_count = 2 * query_count // tile_count
    owner_hits = (owner_tile[:, None] == jnp.arange(tile_count, dtype=jnp.int32)[None, :]).astype(
        jnp.int32
    )
    slot_index = jnp.sum(jnp.cumsum(owner_hits, axis=0) * owner_hits, axis=1) - 1
    base_plane = base_cell // (rows_y * rows_z)
    base_y = base_cell // rows_z % rows_y
    base_z = base_cell % rows_z
    weights = corner_weight(fraction)
    cell_buffer = (
        jnp.zeros((tile_count, 1, slot_count), jnp.int32)
        .at[owner_tile, 0, slot_index]
        .set(base_cell)
    )
    cells_here = lax.all_to_all(cell_buffer, "tile", split_axis=0, concat_axis=0, tiled=True)[:, 0]
    corner_cells = corner_index(
        cells_here // (rows_y * rows_z),
        cells_here // rows_z % rows_y,
        cells_here % rows_z,
        plane_span,
        rows_y,
        rows_z,
    )
    corner_rows = flat_latent[:, corner_cells]
    received = lax.all_to_all(
        jnp.transpose(corner_rows, (2, 0, 1, 3)), "tile", split_axis=0, concat_axis=0, tiled=True
    )
    picked = received[owner_tile, :, :, slot_index]
    interp = jnp.sum(
        picked.astype(jnp.float32) * weights.T.astype(jnp.float32)[:, None, :], axis=2
    ).astype(jnp.bfloat16)
    global_x = owner_tile * plane_list + base_plane
    position = jnp.stack(
        [
            (global_x.astype(jnp.float32) + fraction[0]) / (plane_list * tile_count),
            (base_y.astype(jnp.float32) + fraction[1]) / rows_y,
            (base_z.astype(jnp.float32) + fraction[2]) / rows_z,
        ],
        axis=1,
    )
    target_rows = target[0].T
    query_total = float(query_count * tile_count * replica_count)
    params = (w_latent, w_pos, bias_one, w_mid, bias_two, w_out, bias_out)
    latent_rows = interp.astype(jnp.float32)

    def local_loss(weights_all):
        return point_loss(weights_all, latent_rows, position, target_rows, query_total)

    loss_value, pullback, value = jax.vjp(local_loss, params, has_aux=True)
    gradients = pullback(jnp.ones((), jnp.float32))[0]
    summed = lax.psum(
        (
            gradients[0],
            gradients[1],
            gradients[2],
            gradients[3],
            gradients[4],
            gradients[5],
            gradients[6],
            loss_value,
        ),
        ("replica", "tile"),
    )
    return (
        value.T[None],
        summed[0],
        summed[1],
        summed[2],
        summed[3],
        summed[4],
        summed[5],
        summed[6],
        summed[7],
    )


def solution(mesh):
    return jax.shard_map(
        body,
        mesh=mesh,
        in_specs=(
            P("replica", None, "tile", None, None),
            P(),
            P(),
            P("replica", "tile", None),
            P("replica", "tile"),
            P("replica", None, "tile"),
            P("replica", None, "tile"),
            P(),
            P(),
            P(),
            P(),
            P(),
            P(),
            P(),
        ),
        out_specs=(P("replica", None, "tile"), P(), P(), P(), P(), P(), P(), P(), P()),
        check_vma=False,
    )
```

profile of v0, /device:TPU:8, one launch (start us, length us, event | category | flops | bytes accessed | tf_op | source)
XLA Modules:
  0.0 412.3 jit_solution(445695020267430060)
XLA Ops:
  8.5 3.8 collective-permute-start.1
  14.8 10.9 %scatter_fusion = s32[32,8]{0,1:T(8,128)S(1)} fusion(s32[32,8]{0,1:T(8,128)S(1)} %broadcast.5262, s32[128]{0:T(128)S(1)} %get-tuple-element.71, s32[128]{0:T(128)} %bitcast.586), kind=kCustom, calls=%fused_computation.2 | custom fusion | bytes 2560 | tf_op jit(solution)/shard_map/scatter | solution.py:184
  26.4 6.9 %all-to-all-start = ((s32[32,1,8]{2,1,0:T(1,128)}), s32[32,1,8]{2,1,0:T(1,128)S(1)}, u32[]{:S(2)}, u32[]{:S(2)}) async-start(s32[32,1,8]{2,1,0:T(1,128)} %copy.65), calls=%async_computation | async-start | bytes 32768 | tf_op jit(solution)/shard_map/all_to_all | solution.py:186
  33.6 5.8 %all-to-all-done = s32[32,1,8]{2,1,0:T(1,128)S(1)} async-done(((s32[32,1,8]{2,1,0:T(1,128)}), s32[32,1,8]{2,1,0:T(1,128)S(1)}, u32[]{:S(2)}, u32[]{:S(2)}) %all-to-all-start) | async-done | bytes 1056 | tf_op jit(solution)/shard_map/all_to_all | solution.py:186
  41.4 2.9 fusion.26
  44.3 1.8 fusion.27
  46.1 1.9 fusion.49
  54.5 1.7 fusion.44
  65.9 1.6 collective-permute-start.2
  67.4 2.5 collective-permute-done.2
  71.1 6.2 %gather_fusion = bf16[2048,64]{1,0:T(8,128)(2,1)S(1)} fusion(bf16[64,5120]{0,1:T(8,128)(2,1)S(1)} %bitcast.530, s32[2048]{0:T(1024)S(1)} %broadcast_clamp_fusion), kind=kCustom, calls=%fused_computation | custom fusion | bytes 532480 | tf_op jit(solution)/shard_map/gather | solution.py:195
  79.1 7.7 %all-to-all-start.1 = ((bf16[32,2,2048]{2,1,0:T(2,128)(2,1)}), bf16[32,2,2048]{2,1,0:T(2,128)(2,1)S(1)}, u32[]{:S(2)}, u32[]{:S(2)}) async-start(bf16[32,2,2048]{2,1,0:T(2,128)(2,1)} %reshape.1907), calls=%async_computation.1 | async-start | bytes 524288 | tf_op jit(solution)/shard_map/all_to_all | solution.py:196
  87.5 6.8 %all-to-all-done.1 = bf16[32,2,2048]{2,1,0:T(2,128)(2,1)S(1)} async-done(((bf16[32,2,2048]{2,1,0:T(2,128)(2,1)}), bf16[32,2,2048]{2,1,0:T(2,128)(2,1)S(1)}, u32[]{:S(2)}, u32[]{:S(2)}) %all-to-all-start.1) | async-done | bytes 262176 | tf_op jit(solution)/shard_map/all_to_all | solution.py:196
  98.3 2.2 copy.81
  100.5 4.5 %fusion.213 = f32[896,512]{1,0:T(8,128)S(1)} fusion(f32[896,512]{1,0:T(8,128)} %bitcast.538, f32[512,512]{1,0:T(8,128)S(1)} %copy-done), kind=kOutput, calls=%fused_computation.422 | convolution fusion | flops 2818572288 | bytes 4718592 | tf_op jit(solution)/shard_map/jvp()/dot_general | solution.py:86
  108.0 1.6 fusion.214
  112.5 1.6 fusion.113
  117.5 3.1 fusion.215
  120.5 1.3 fusion.200
  121.8 2.3 copy.82
  124.1 1.9 multiply_reduce_fusion.1
  126.0 6.4 %convolution_bitcast_fusion.13 = f32[512,512]{1,0:T(8,128)} fusion(f32[1,128,512]{2,1,0:T(8,128)} %bitcast.580, f32[3,128,512]{2,1,0:T(8,128)} %copy-done.10, f32[3,128,512]{2,1,0:T(8,128)} %copy-done.11, f32[3,128,512]{1,2,0:T(8,128)} %copy-done.9, f32[3,128,512]{1,2,0:T(8,128)} %copy-done.8, f32[1,128,512]{1,2,0:T(8,128)} %copy-done.17), kind=kOutput, calls=%fused_computation.60 | convolution fusion | flops 2820407296 | bytes 4718592 | tf_op jit(solution)/shard_map/transpose(jvp())/dot_general | solution.py:86
  132.4 2.3 copy.84
  134.7 2.8 fusion.37
  137.5 1.8 copy.83
  139.2 1.8 copy.85
  141.1 1.4 fusion.197
  144.7 2.3 convolution_bitcast_fusion.14
  147.3 77.7 %all-reduce.25 = (f32[3,512]{1,0:T(4,128)}, f32[512]{0:T(512)}, f32[512]{0:T(512)}, f32[5,512]{1,0:T(8,128)}, f32[5]{0:T(128)}, /*index=5*/f32[]{:T(128)}) all-reduce(f32[3,512]{1,0:T(4,128)S(1)} %convolution_add_fusion.14, f32[512]{0:T(512)S(1)} %get-tuple-element.67, ...), channel_id=1, replica_groups=mesh['replica'=8,'tile'=32] {'replica','tile'}, use_global_device_ids=true, to_apply=%region_15.16 | all-reduce | flops 5126 | bytes 41008 | tf_op jit(solution)/shard_map/psum | solution.py:222
  225.0 176.5 %all-reduce.29.cloned.1.call-done = (f32[64,512]{1,0:T(8,128)}, f32[512,512]{1,0:T(8,128)}) async-done(((f32[64,512]{1,0:T(8,128)}, f32[512,512]{1,0:T(8,128)}), (f32[64,512]{1,0:T(8,128)}, f32[512,512]{1,0:T(8,128)})) %all-reduce.29.cloned.1.call-update) | async-done | bytes 1179664 | tf_op jit(solution)/shard_map/psum | solution.py:222
  401.4 1.6 copy.245
  403.0 2.3 copy.246
  (200 shorter events, 40.5 us)
Async XLA Ops:
  7.2 93.3 %copy-start = (f32[512,512]{1,0:T(8,128)S(1)}, f32[512,512]{1,0:T(8,128)}, u32[]{:S(2)}) copy-start(f32[512,512]{1,0:T(8,128)} %param.24) | copy-start | bytes 3145732
  7.2 26.2 %copy-start.1 = (bf16[1,64,4,8,128]{4,3,2,1,0:T(8,128)(2,1)S(1)}, bf16[1,64,4,8,128]{4,3,2,1,0:T(8,128)(2,1)}, u32[]{:S(2)}) copy-start(bf16[1,64,4,8,128]{4,3,2,1,0:T(8,128)(2,1)} %param.14) | copy-start | bytes 1572868
  7.2 26.1 %copy-start.25 = (f32[1,3,128]{2,0,1:T(1,128)S(1)}, f32[1,3,128]{2,0,1:T(1,128)}, u32[]{:S(2)}) copy-start(f32[1,3,128]{2,0,1:T(1,128)} %param.19) | copy-start | bytes 4612
  8.4 32.0 %collective-permute-start = (bf16[64,2,8,128]{3,2,1,0:T(8,128)(2,1)S(1)}, bf16[64,2,8,128]{3,2,1,0:T(8,128)(2,1)S(1)}, u32[]{:S(2)}, u32[]{:S(2)}) collective-permute-start(bf16[64,2,8,128]{3,2,1,0:T(8,128)(2,1)S(1)} %get-tuple-element.124), channel_id=1, source_target_pairs={{0,1},{1,2},{2,3},{3,4},{4,5},{5,6},{6,7},{7,8},{8,9},{9,10},{10,1... | collective-permute-start | bytes 786440 | tf_op jit(solution)/shard_map/ppermute | solution.py:19
  8.5 31.9 %collective-permute-start.1 = (bf16[64,2,8,128]{3,2,1,0:T(8,128)(2,1)S(1)}, bf16[64,2,8,128]{3,2,1,0:T(8,128)(2,1)S(1)}, u32[]{:S(2)}, u32[]{:S(2)}) collective-permute-start(bf16[64,2,8,128]{3,2,1,0:T(8,128)(2,1)S(1)} %get-tuple-element.125), channel_id=1, source_target_pairs={{1,0},{2,1},{3,2},{4,3},{5,4},{6,5},{7,6},{8,7},{9,8},{10,9},{11,1... | collective-permute-start | bytes 786440 | tf_op jit(solution)/shard_map/ppermute | solution.py:21
  26.4 13.1 %all-to-all-start = ((s32[32,1,8]{2,1,0:T(1,128)}), s32[32,1,8]{2,1,0:T(1,128)S(1)}, u32[]{:S(2)}, u32[]{:S(2)}) async-start(s32[32,1,8]{2,1,0:T(1,128)} %copy.65), calls=%async_computation | async-start | bytes 32768 | tf_op jit(solution)/shard_map/all_to_all | solution.py:186
  50.3 0.9 copy-start.21
  65.9 4.1 collective-permute-start.2
  77.3 9.6 %copy-start.27 = (s32[1,128,1]{1,2,0:T(1,128)S(1)}, s32[1,128,1]{1,2,0:T(1,128)}, u32[]{:S(2)}) copy-start(s32[1,128,1]{1,2,0:T(1,128)} %param.17) | copy-start | bytes 1540
  77.3 9.5 %copy-start.31 = (s32[1,128]{1,0:T(1,128)S(1)}, s32[1,128]{1,0:T(1,128)}, u32[]{:S(2)}) copy-start(s32[1,128]{1,0:T(1,128)} %param.18) | copy-start | bytes 1540
  77.4 9.7 %copy-start.23 = (f32[3,512]{1,0:T(4,128)S(1)}, f32[3,512]{1,0:T(4,128)}, u32[]{:S(2)}) copy-start(f32[3,512]{1,0:T(4,128)} %param.22) | copy-start | bytes 18436
  79.1 15.2 %all-to-all-start.1 = ((bf16[32,2,2048]{2,1,0:T(2,128)(2,1)}), bf16[32,2,2048]{2,1,0:T(2,128)(2,1)S(1)}, u32[]{:S(2)}, u32[]{:S(2)}) async-start(bf16[32,2,2048]{2,1,0:T(2,128)(2,1)} %reshape.1907), calls=%async_computation.1 | async-start | bytes 524288 | tf_op jit(solution)/shard_map/all_to_all | solution.py:196
  86.8 314.6 %all-reduce.29.cloned.1.call-start = ((), (), s32[]{:S(2)}) async-start(), calls=%async_computation.2 | async-start | bytes 2359296 | tf_op jit(solution)/shard_map/psum | solution.py:222
  94.7 1.2 copy-start.22
  94.7 1.2 copy-start.30
  96.7 1.6 copy-start.17
  97.0 1.1 copy-start.9
  105.7 1.1 copy-start.4
  105.8 1.1 copy-start.18
  106.8 0.9 copy-start.6
  106.8 1.2 copy-start.7
  106.9 1.1 copy-start.24
  108.0 1.6 copy-start.28
  108.0 3.6 copy-start.29
  114.2 1.1 copy-start.3
  114.2 1.4 copy-start.5
  116.1 0.9 copy-start.10
  116.1 1.2 copy-start.11
  116.3 1.1 copy-start.20
  126.0 8.7 %copy-start.13 = (f32[128,512]{0,1:T(8,128)S(1)}, f32[128,512]{0,1:T(8,128)}, u32[]{:S(2)}) copy-start(f32[128,512]{0,1:T(8,128)} %copy-done.12) | copy-start | bytes 786436
  126.0 8.7 %copy-start.15 = (f32[128,512]{0,1:T(8,128)S(1)}, f32[128,512]{0,1:T(8,128)}, u32[]{:S(2)}) copy-start(f32[128,512]{0,1:T(8,128)} %copy-done.14) | copy-start | bytes 786436
  139.2 5.4 %copy-start.19 = (f32[1,128,512]{2,1,0:T(8,128)S(1)}, f32[1,128,512]{2,1,0:T(8,128)}, u32[]{:S(2)}) copy-start(f32[1,128,512]{2,1,0:T(8,128)} %copy-done.18) | copy-start | bytes 786436
  (7 other events, 5.4 us)
Sparse Core Ops, SparseCore 0:
  143.5 257.9 all-reduce.28
where the time goes:
time: 420 us; the launch traced here: 412 us
  waiting for transfers between devices  192 us (46%)
  blocking collectives  77.7 us (18%)
  local copies, waits for them, and re-layouts  50.4 us (12%)
  matrix products  31.4 us (7%)
  other arithmetic  25 us (6%)
  starting transfers between devices  20.2 us (5%)
  between operations  15.9 us (4%)
    psum x1, waiting for transfers between devices, body(): lax.psum((gradients[0], gradients[1], gradients[2], gradients[3], gradien...  176 us
    psum x1, blocking collectives, body(): lax.psum((gradients[0], gradients[1], gradients[2], gradients[3], gradien...  77.7 us
    dot_general x3, matrix products, decode(): jnp.dot(stacked, w_mid, precision=highest)  14 us
    concatenate x8, other arithmetic, convolved_tile(): jnp.roll(padded_field, (-spacing_along_y, -spacing_along_z), axis=(2, 3))  12.2 us
    unnamed x79, local copies, waits for them, and re-layouts  12 us
    scatter x2, local copies, waits for them, and re-layouts, body(): cell_buffer = jnp.zeros((tile_count, 1, slot_count), jnp.int32).at[owner_...  11.6 us
    dot_general x27, matrix products, convolved_tile(): jnp.dot(convolution_weight[:, tap_index * channels:(tap_index + 1) * chan...  9.92 us
  transfers between devices with their start and end apart: 6, of which 4 were waited for; matrix products, arithmetic and copies ran while one was open for 5% of the time, Pallas kernels for 0%

commit v1 on v0

--- a/solution.py
+++ b/solution.py
@@ -7,6 +7,11 @@
 VISCOSITY = 0.05
 DIFFUSIVITY = 0.05
 RESIDUAL_WEIGHT = 0.5
+
+
+def axis_by_axis(value_2, first, second_2):
+    partial = lax.psum(value_2, first)
+    return lax.psum(partial, second_2)
 
 
 def extended_2(cells, sides, width):
@@ -219,7 +224,7 @@
 
     loss_value, pullback, value = jax.vjp(local_loss, params, has_aux=True)
     gradients = pullback(jnp.ones((), jnp.float32))[0]
-    summed = lax.psum(
+    summed = axis_by_axis(
         (
             gradients[0],
             gradients[1],
@@ -230,7 +235,8 @@
             gradients[6],
             loss_value,
         ),
-        ("replica", "tile"),
+        "replica",
+        "tile",
     )
     return (
         value.T[None],

time: 420 us -> 391 us (0.931)
  the two profiles are of different devices: /device:TPU:8 before, /device:TPU:0 now
where the time goes in v1:
time: 391 us; the launch traced here: 384 us
  blocking collectives  153 us (39%)
  waiting for transfers between devices  92.2 us (24%)
  local copies, waits for them, and re-layouts  50.4 us (13%)
  matrix products  30.1 us (8%)
  other arithmetic  25 us (6%)
  starting transfers between devices  17.2 us (4%)
  between operations  15.9 us (4%)
    psum x1, blocking collectives, axis_by_axis(): return lax.psum(partial, second_2)  124 us
    psum x1, waiting for transfers between devices, axis_by_axis(): partial = lax.psum(value_2, first)  74.5 us
    psum x1, blocking collectives, axis_by_axis(): partial = lax.psum(value_2, first)  29.2 us
    dot_general x3, matrix products, decode(): jnp.dot(stacked, w_mid, precision=highest)  14 us
    concatenate x8, other arithmetic, convolved_tile(): jnp.roll(padded_field, (-spacing_along_y, -spacing_along_z), axis=(2, 3))  12.2 us
    unnamed x83, local copies, waits for them, and re-layouts  12 us
    scatter x2, local copies, waits for them, and re-layouts, body(): cell_buffer = jnp.zeros((tile_count, 1, slot_count), jnp.int32).at[owner_...  11.6 us
    dot_general x27, matrix products, convolved_tile(): jnp.dot(convolution_weight[:, tap_index * channels:(tap_index + 1) * chan...  9.93 us
  transfers between devices with their start and end apart: 7, of which 4 were waited for; matrix products, arithmetic and copies ran while one was open for 5% of the time, Pallas kernels for 0%

profile of v1, /device:TPU:0, one launch (start us, length us, event | category | flops | bytes accessed | tf_op | source)
XLA Modules:
  0.0 383.9 jit_solution(4062163821619677312)
XLA Ops:
  8.5 5.1 %collective-permute-start.1 = (bf16[64,2,8,128]{3,2,1,0:T(8,128)(2,1)S(1)}, bf16[64,2,8,128]{3,2,1,0:T(8,128)(2,1)S(1)}, u32[]{:S(2)}, u32[]{:S(2)}) collective-permute-start(bf16[64,2,8,128]{3,2,1,0:T(8,128)(2,1)S(1)} %get-tuple-element.133), channel_id=1, source_target_pairs={{1,0},{2,1},{3,2},{4,3},{5,4},{6,5},{7,6},{8,7},{9,8},{10,9},{11,1... | collective-permute-start | bytes 786440 | tf_op jit(solution)/shard_map/ppermute | solution.py:26
  16.0 10.9 %scatter_fusion = s32[32,8]{0,1:T(8,128)S(1)} fusion(s32[32,8]{0,1:T(8,128)S(1)} %broadcast.5262, s32[128]{0:T(128)S(1)} %get-tuple-element.79, s32[128]{0:T(128)} %bitcast.586), kind=kCustom, calls=%fused_computation.2 | custom fusion | bytes 2560 | tf_op jit(solution)/shard_map/scatter | solution.py:189
  27.6 3.8 all-to-all-start
  31.8 7.0 %all-to-all-done = s32[32,1,8]{2,1,0:T(1,128)S(1)} async-done(((s32[32,1,8]{2,1,0:T(1,128)}), s32[32,1,8]{2,1,0:T(1,128)S(1)}, u32[]{:S(2)}, u32[]{:S(2)}) %all-to-all-start) | async-done | bytes 1056 | tf_op jit(solution)/shard_map/all_to_all | solution.py:191
  40.6 2.9 fusion.26
  43.5 1.8 fusion.27
  45.3 1.9 fusion.49
  53.7 1.7 fusion.44
  65.1 1.3 collective-permute-start.2
  66.4 2.5 collective-permute-done.2
  70.1 6.2 %gather_fusion = bf16[2048,64]{1,0:T(8,128)(2,1)S(1)} fusion(bf16[64,5120]{0,1:T(8,128)(2,1)S(1)} %bitcast.530, s32[2048]{0:T(1024)S(1)} %broadcast_clamp_fusion), kind=kCustom, calls=%fused_computation | custom fusion | bytes 532480 | tf_op jit(solution)/shard_map/gather | solution.py:200
  78.0 6.8 %all-to-all-start.1 = ((bf16[32,2,2048]{2,1,0:T(2,128)(2,1)}), bf16[32,2,2048]{2,1,0:T(2,128)(2,1)S(1)}, u32[]{:S(2)}, u32[]{:S(2)}) async-start(bf16[32,2,2048]{2,1,0:T(2,128)(2,1)} %reshape.1907), calls=%async_computation.1 | async-start | bytes 524288 | tf_op jit(solution)/shard_map/all_to_all | solution.py:201
  85.5 8.3 %all-to-all-done.1 = bf16[32,2,2048]{2,1,0:T(2,128)(2,1)S(1)} async-done(((bf16[32,2,2048]{2,1,0:T(2,128)(2,1)}), bf16[32,2,2048]{2,1,0:T(2,128)(2,1)S(1)}, u32[]{:S(2)}, u32[]{:S(2)}) %all-to-all-start.1) | async-done | bytes 262176 | tf_op jit(solution)/shard_map/all_to_all | solution.py:201
  97.8 2.2 copy.81
  100.0 4.5 %fusion.213 = f32[896,512]{1,0:T(8,128)S(1)} fusion(f32[896,512]{1,0:T(8,128)} %bitcast.538, f32[512,512]{1,0:T(8,128)S(1)} %copy-done), kind=kOutput, calls=%fused_computation.422 | convolution fusion | flops 2818572288 | bytes 4718592 | tf_op jit(solution)/shard_map/jvp()/dot_general | solution.py:91
  107.5 1.6 fusion.214
  112.0 1.6 fusion.113
  116.9 3.1 fusion.215
  120.0 1.3 fusion.200
  121.2 2.3 copy.82
  123.5 1.9 multiply_reduce_fusion.1
  125.4 6.4 %convolution_bitcast_fusion.13 = f32[512,512]{1,0:T(8,128)} fusion(f32[1,128,512]{2,1,0:T(8,128)} %bitcast.580, f32[3,128,512]{2,1,0:T(8,128)} %copy-done.12, f32[3,128,512]{2,1,0:T(8,128)} %copy-done.13, f32[3,128,512]{1,2,0:T(8,128)} %copy-done.11, f32[3,128,512]{1,2,0:T(8,128)} %copy-done.10, f32[1,128,512]{1,2,0:T(8,128)} %copy-done.19), kind=kOutput, calls=%fused_computation.60 | convolution fusion | flops 2820407296 | bytes 4718592 | tf_op jit(solution)/shard_map/transpose(jvp())/dot_general | solution.py:91
  131.8 2.3 copy.84
  134.1 2.8 fusion.37
  136.9 1.8 copy.83
  138.7 1.8 copy.85
  140.5 1.4 fusion.197
  142.9 74.5 %all-reduce.34.cloned.1.call-done = (f32[64,512]{1,0:T(8,128)}, f32[512,512]{1,0:T(8,128)}) async-done(((f32[64,512]{1,0:T(8,128)}, f32[512,512]{1,0:T(8,128)}), (f32[64,512]{1,0:T(8,128)}, f32[512,512]{1,0:T(8,128)})) %all-reduce.34.cloned.1.call-update) | async-done | bytes 1179664 | tf_op jit(solution)/shard_map/psum | solution.py:13
  219.9 29.2 %all-reduce.27 = (f32[3,512]{1,0:T(4,128)S(1)}, f32[512]{0:T(512)S(1)}, f32[512]{0:T(512)S(1)}, f32[5,512]{1,0:T(8,128)S(1)}, f32[5]{0:T(128)S(1)}, /*index=5*/f32[]{:T(128)}) all-reduce(f32[3,512]{1,0:T(4,128)S(1)} %convolution_add_fusion.14, f32[512]{0:T(512)S(1)} %get-tuple-element.75, ...), channel_id=1, replica_groups=mesh['replica'=8,'tile'=32] {'replica'}, use_global_device_ids=true, to_apply=%region_16.17 | all-reduce | flops 5126 | bytes 41008 | tf_op jit(solution)/shard_map/psum | solution.py:13
  249.1 123.9 %all-reduce.25 = (f32[3,512]{1,0:T(4,128)}, f32[512]{0:T(512)}, f32[512]{0:T(512)}, f32[5,512]{1,0:T(8,128)}, f32[5]{0:T(128)}, /*index=5*/f32[]{:T(128)}) all-reduce(f32[3,512]{1,0:T(4,128)S(1)} %get-tuple-element.61, f32[512]{0:T(512)S(1)} %get-tuple-element.62, ...), channel_id=1, replica_groups=mesh['replica'=8,'tile'=32] {'tile'}, use_global_device_ids=true, to_apply=%region_17.18 | all-reduce | flops 5126 | bytes 41008 | tf_op jit(solution)/shard_map/psum | solution.py:14
  373.0 1.6 copy.247
  374.6 2.3 copy.248
  (208 shorter events, 41.5 us)
Async XLA Ops:
  7.2 92.8 %copy-start = (f32[512,512]{1,0:T(8,128)S(1)}, f32[512,512]{1,0:T(8,128)}, u32[]{:S(2)}) copy-start(f32[512,512]{1,0:T(8,128)} %param.24) | copy-start | bytes 3145732
  7.2 24.3 %copy-start.1 = (bf16[1,64,4,8,128]{4,3,2,1,0:T(8,128)(2,1)S(1)}, bf16[1,64,4,8,128]{4,3,2,1,0:T(8,128)(2,1)}, u32[]{:S(2)}) copy-start(bf16[1,64,4,8,128]{4,3,2,1,0:T(8,128)(2,1)} %param.14) | copy-start | bytes 1572868
  7.2 24.2 %copy-start.27 = (f32[1,3,128]{2,0,1:T(1,128)S(1)}, f32[1,3,128]{2,0,1:T(1,128)}, u32[]{:S(2)}) copy-start(f32[1,3,128]{2,0,1:T(1,128)} %param.19) | copy-start | bytes 4612
  8.4 31.2 %collective-permute-start = (bf16[64,2,8,128]{3,2,1,0:T(8,128)(2,1)S(1)}, bf16[64,2,8,128]{3,2,1,0:T(8,128)(2,1)S(1)}, u32[]{:S(2)}, u32[]{:S(2)}) collective-permute-start(bf16[64,2,8,128]{3,2,1,0:T(8,128)(2,1)S(1)} %get-tuple-element.132), channel_id=1, source_target_pairs={{0,1},{1,2},{2,3},{3,4},{4,5},{5,6},{6,7},{7,8},{8,9},{9,10},{10,1... | collective-permute-start | bytes 786440 | tf_op jit(solution)/shard_map/ppermute | solution.py:24
  8.5 31.1 %collective-permute-start.1 = (bf16[64,2,8,128]{3,2,1,0:T(8,128)(2,1)S(1)}, bf16[64,2,8,128]{3,2,1,0:T(8,128)(2,1)S(1)}, u32[]{:S(2)}, u32[]{:S(2)}) collective-permute-start(bf16[64,2,8,128]{3,2,1,0:T(8,128)(2,1)S(1)} %get-tuple-element.133), channel_id=1, source_target_pairs={{1,0},{2,1},{3,2},{4,3},{5,4},{6,5},{7,6},{8,7},{9,8},{10,9},{11,1... | collective-permute-start | bytes 786440 | tf_op jit(solution)/shard_map/ppermute | solution.py:26
  27.6 11.1 %all-to-all-start = ((s32[32,1,8]{2,1,0:T(1,128)}), s32[32,1,8]{2,1,0:T(1,128)S(1)}, u32[]{:S(2)}, u32[]{:S(2)}) async-start(s32[32,1,8]{2,1,0:T(1,128)} %copy.65), calls=%async_computation | async-start | bytes 32768 | tf_op jit(solution)/shard_map/all_to_all | solution.py:191
  65.1 3.8 collective-permute-start.2
  76.3 8.7 %copy-start.29 = (s32[1,128,1]{1,2,0:T(1,128)S(1)}, s32[1,128,1]{1,2,0:T(1,128)}, u32[]{:S(2)}) copy-start(s32[1,128,1]{1,2,0:T(1,128)} %param.17) | copy-start | bytes 1540
  76.3 8.7 %copy-start.33 = (s32[1,128]{1,0:T(1,128)S(1)}, s32[1,128]{1,0:T(1,128)}, u32[]{:S(2)}) copy-start(s32[1,128]{1,0:T(1,128)} %param.18) | copy-start | bytes 1540
  76.3 8.8 %copy-start.25 = (f32[3,512]{1,0:T(4,128)S(1)}, f32[3,512]{1,0:T(4,128)}, u32[]{:S(2)}) copy-start(f32[3,512]{1,0:T(4,128)} %param.22) | copy-start | bytes 18436
  78.0 15.8 %all-to-all-start.1 = ((bf16[32,2,2048]{2,1,0:T(2,128)(2,1)}), bf16[32,2,2048]{2,1,0:T(2,128)(2,1)S(1)}, u32[]{:S(2)}, u32[]{:S(2)}) async-start(bf16[32,2,2048]{2,1,0:T(2,128)(2,1)} %reshape.1907), calls=%async_computation.1 | async-start | bytes 524288 | tf_op jit(solution)/shard_map/all_to_all | solution.py:201
  84.9 132.5 %all-reduce.34.cloned.1.call-start = ((), (), s32[]{:S(2)}) async-start(), calls=%async_computation.3 | async-start | bytes 2359296 | tf_op jit(solution)/shard_map/psum | solution.py:13
  94.1 1.2 copy-start.24
  94.1 1.2 copy-start.32
  96.2 1.6 copy-start.19
  96.5 1.2 copy-start.11
  105.2 1.1 copy-start.4
  105.3 1.1 copy-start.20
  106.4 1.1 copy-start.8
  106.4 1.1 copy-start.26
  107.5 1.6 copy-start.30
  107.5 3.6 copy-start.31
  113.7 1.1 copy-start.3
  113.7 1.4 copy-start.5
  115.6 1.1 copy-start.13
  115.8 1.1 copy-start.22
  125.4 8.7 %copy-start.15 = (f32[128,512]{0,1:T(8,128)S(1)}, f32[128,512]{0,1:T(8,128)}, u32[]{:S(2)}) copy-start(f32[128,512]{0,1:T(8,128)} %copy-done.14) | copy-start | bytes 786436
  125.4 8.7 %copy-start.17 = (f32[128,512]{0,1:T(8,128)S(1)}, f32[128,512]{0,1:T(8,128)}, u32[]{:S(2)}) copy-start(f32[128,512]{0,1:T(8,128)} %copy-done.16) | copy-start | bytes 786436
  140.5 78.2 %copy-start.21 = (f32[1,128,512]{2,1,0:T(8,128)S(1)}, f32[1,128,512]{2,1,0:T(8,128)}, u32[]{:S(2)}) copy-start(f32[1,128,512]{2,1,0:T(8,128)} %copy-done.20) | copy-start | bytes 786436
  141.9 76.8 %copy-start.7 = (f32[3,128,512]{2,1,0:T(8,128)S(1)}, f32[3,128,512]{2,1,0:T(8,128)}, u32[]{:S(2)}) copy-start(f32[3,128,512]{2,1,0:T(8,128)} %copy-done.6) | copy-start | bytes 2359300
  141.9 76.8 %copy-start.9 = (f32[3,128,512]{2,1,0:T(8,128)S(1)}, f32[3,128,512]{2,1,0:T(8,128)}, u32[]{:S(2)}) copy-start(f32[3,128,512]{2,1,0:T(8,128)} %copy-done.8) | copy-start | bytes 2359300
  142.8 230.2 %all-reduce.32.cloned.1.call-start = ((), (), s32[]{:S(2)}) async-start(), calls=%async_computation.2 | async-start | bytes 2359296 | tf_op jit(solution)/shard_map/psum | solution.py:14
  (10 other events, 8.1 us)
Sparse Core Ops, SparseCore 0:
  143.0 74.3 all-reduce.33
  220.7 113.7 all-reduce.31
